TPU v7x, 256 devices: a whole 4x4x8 slice. The times are simulated.
256 devices in a mesh: tm: 32 (over z_lo, x, core), cells: 8 (over y, z_hi).
Axes of the slice: x: 4, y: 4, z: 8 (z_hi: 2, z_lo: 4; z = z_hi * 4 + z_lo), core: 2. Of those that a mesh axis runs over, the one named last changes fastest.
Arguments:
- hist_bin: int32 [16384, 8192], P('tm', 'cells'), may hold values from 0 to 255
- obs_bin: int32 [16384, 8192], P('tm', 'cells'), may hold values from 0 to 255
- fut_bin: int32 [16384, 8192], P('tm', 'cells'), may hold values from 0 to 255
- region_id: int32 [8192], P('cells'), may hold values from 0 to 127, as said below
- bin_width: float32 [8192], P('cells'), may hold values from 0.005 to 0.05
- bin_offset: float32 [8192], P('cells'), may hold values from -4 to 4
Outputs:
- adjusted: float32 [16384, 8192], P('tm', 'cells')
Inputs may be any that keep to these rules, and one draw needn't show every extreme that they name: `region_id`: every zone of 0 to 127 holds exactly 64 cells.
All inputs are finite; a program needn't handle non-finite values.
Results may differ from a plain program's by a relative error of at most 0.0003.
Values sent between devices are 32-bit elements; how exact they have to be, the bound alone decides.
A program may use at most 64 MiB of HBM per device.

v0:
```python
import math
import jax
import jax.numpy as jnp
from jax import lax
from jax.sharding import PartitionSpec as P

BINS = 256
REGIONS = 128
pool_weight = 0.5


def in_order(blocks, dim):
    blocks = jnp.moveaxis(blocks, 0, dim)
    dims = blocks.shape
    return blocks.reshape(*dims[:dim], dims[dim] * dims[dim + 1], *dims[dim + 2 :])


def copy_for_each(array, axis):
    count = lax.axis_size(axis)
    return lax.all_to_all(
        jnp.broadcast_to(array[None], (count, *array.shape)), axis, 0, 0, tiled=True
    )


def collect(array, axis, dim):
    return in_order(copy_for_each(array, axis), dim)


def tally_bins(stacked, levels):
    series, day_count, cell_count = stacked.shape
    day_block = math.gcd(day_count, max(1, 16384 // cell_count))

    def add_block(turn_index, totals):
        portion = lax.dynamic_slice_in_dim(stacked, turn_index * day_block, day_block, 1)
        matches = (portion[..., None] == levels).astype(jnp.bfloat16)
        return totals + jnp.sum(matches, axis=1, dtype=jnp.float32)

    initial = jnp.zeros((series, cell_count, levels.shape[0]), jnp.float32)
    return lax.fori_loop(0, day_count // day_block, add_block, initial)


def quantile_at(rank_rows, before_rows, pooled_rows):
    ramp_terms = jnp.minimum(
        jnp.maximum(rank_rows[:, :, None] - before_rows[:, None, :], 0.0), pooled_rows[:, None, :]
    )
    return jnp.sum(ramp_terms / jnp.maximum(pooled_rows, 1.0)[:, None, :], axis=2)


def build_table(totals, zone_rows, zone_share, widths, offsets, day_total):
    zone_terms = jnp.einsum(
        "cr,srb->scb",
        zone_rows,
        zone_share,
        precision=lax.Precision.HIGHEST,
        preferred_element_type=jnp.float32,
    )
    pooled = totals + pool_weight * day_total * zone_terms
    bins_total = pooled.shape[2]
    ladder = jnp.arange(bins_total, dtype=jnp.int32)
    upper_mask = (ladder[:, None] <= ladder[None, :]).astype(jnp.float32)
    running = jnp.einsum(
        "scb,bd->scd",
        pooled,
        upper_mask,
        precision=lax.Precision.HIGHEST,
        preferred_element_type=jnp.float32,
    )
    before = running - pooled
    future_rank = before[2] + 0.5 * pooled[2]
    row_count = pooled.shape[1]
    group_size = math.gcd(row_count, 128)
    group_count = row_count // group_size

    def per_group(group_rows):
        rank_rows, obs_before, obs_pooled, hist_before, hist_pooled = group_rows
        return (
            quantile_at(rank_rows, obs_before, obs_pooled),
            quantile_at(rank_rows, hist_before, hist_pooled),
        )

    shaped = (
        future_rank.reshape(group_count, group_size, bins_total),
        before[1].reshape(group_count, group_size, bins_total),
        pooled[1].reshape(group_count, group_size, bins_total),
        before[0].reshape(group_count, group_size, bins_total),
        pooled[0].reshape(group_count, group_size, bins_total),
    )
    quant_obs, quant_hist = lax.map(per_group, shaped)
    quant_obs = quant_obs.reshape(row_count, bins_total)
    quant_hist = quant_hist.reshape(row_count, bins_total)
    centers = (ladder.astype(jnp.float32) + 0.5)[None, :]
    return offsets[:, None] + widths[:, None] * (centers + quant_obs - quant_hist)


def apply_table(fut_bin, lookup, levels):
    day_count, cell_count = fut_bin.shape
    day_block = math.gcd(day_count, max(1, 16384 // cell_count))
    folded = fut_bin.reshape(day_count // day_block, day_block, cell_count)

    def select_rows(bins_rows):
        matches = bins_rows[..., None] == levels
        return jnp.sum(jnp.where(matches, lookup[None], 0.0), axis=2)

    return lax.map(select_rows, folded).reshape(day_count, cell_count)


def body(hist_bin, obs_bin, fut_bin, region_id, bin_width, bin_offset):
    day_count, cell_count = hist_bin.shape
    levels = jnp.arange(BINS, dtype=jnp.int32)
    stacked = jnp.stack([hist_bin, obs_bin, fut_bin])
    totals = tally_bins(stacked, levels)
    zone_rows = (region_id[:, None] == jnp.arange(REGIONS, dtype=jnp.int32)[None, :]).astype(
        jnp.float32
    )
    zone_part = jnp.einsum(
        "cr,scb->srb",
        zone_rows,
        totals,
        precision=lax.Precision.HIGHEST,
        preferred_element_type=jnp.float32,
    )
    zone_counts = lax.psum(zone_part, ("tm", "cells"))
    zone_share = zone_counts / jnp.sum(zone_counts, axis=2, keepdims=True)
    day_total = day_count * lax.axis_size("tm")
    share_rows = lax.psum_scatter(totals, "tm", scatter_dimension=1, tiled=True)
    share_count = share_rows.shape[1]
    first_row = lax.axis_index("tm") * share_count
    share_zones = lax.dynamic_slice_in_dim(zone_rows, first_row, share_count, 0)
    share_widths = lax.dynamic_slice_in_dim(bin_width, first_row, share_count, 0)
    share_offsets = lax.dynamic_slice_in_dim(bin_offset, first_row, share_count, 0)
    partial_table = build_table(
        share_rows, share_zones, zone_share, share_widths, share_offsets, day_total
    )
    lookup = collect(partial_table, "tm", 0)
    return apply_table(fut_bin, lookup, levels)


def solution(mesh):
    placed = (
        P("tm", "cells"),
        P("tm", "cells"),
        P("tm", "cells"),
        P("cells"),
        P("cells"),
        P("cells"),
    )
    return jax.shard_map(
        body, mesh=mesh, in_specs=placed, out_specs=P("tm", "cells"), check_vma=False
    )
```

profile of v0, /device:TPU:1, one launch (start us, length us, event | category | flops | bytes accessed | tf_op | source)
XLA Modules:
  0.0 995.9 jit_solution(16803068548199994457)
XLA Ops:
  14.0 453.7 %while.31 = (s32[]{:T(128)}, f32[3,1024,256]{2,1,0:T(8,128)}, s32[3,512,1024]{2,1,0:T(8,128)}, s32[]{:T(128)}, s32[]{:T(128)}, /*index=5*/s32[]{:T(128)}, s32[]{:T(128)}) while((s32[]{:T(128)}, f32[3,1024,256]{2,1,0:T(8,128)}, s32[3,512,1024]{2,1,0:T(8,128)}, s32[]{:T(128)}, s32[]{:T(128)}, /*index=5*/s32[]{:T(128)}, ...), condition=%wide.region_2.0_spmd.clone, body=%wide.region_0.0_spmd.clone.sunk | while | flops 51118084 | bytes 13172873 | solution.py:39
  15.0 9.3 convert_reduce_fusion.2
  27.3 9.3 convert_reduce_fusion.2
  41.6 9.3 convert_reduce_fusion.2
  55.8 9.3 convert_reduce_fusion.2
  70.0 9.3 convert_reduce_fusion.2
  84.3 9.3 convert_reduce_fusion.2
  98.5 9.3 convert_reduce_fusion.2
  112.7 9.3 convert_reduce_fusion.2
  127.0 9.3 convert_reduce_fusion.2
  141.2 9.3 convert_reduce_fusion.2
  155.5 9.3 convert_reduce_fusion.2
  169.7 9.3 convert_reduce_fusion.2
  183.9 9.3 convert_reduce_fusion.2
  198.2 9.3 convert_reduce_fusion.2
  212.4 9.3 convert_reduce_fusion.2
  226.6 9.3 convert_reduce_fusion.2
  240.9 9.3 convert_reduce_fusion.2
  255.1 9.3 convert_reduce_fusion.2
  269.4 9.3 convert_reduce_fusion.2
  283.6 9.3 convert_reduce_fusion.2
  475.5 253.2 %all-reduce.2.cloned.1.call-done = f32[3,128,256]{1,2,0:T(8,128)} async-done(((f32[3,128,256]{1,2,0:T(8,128)}), f32[3,128,256]{1,2,0:T(8,128)}) %all-reduce.2.cloned.1.call-update) | async-done | bytes 393232 | tf_op jit(solution)/shard_map/psum | solution.py:122
  742.8 26.6 %all-to-all-done = f32[32,32,256]{2,1,0:T(8,128)S(1)} async-done(((f32[32,32,256]{2,1,0:T(8,128)}), f32[32,32,256]{2,1,0:T(8,128)S(1)}, u32[]{:S(2)}, u32[]{:S(2)}) %all-to-all-start) | async-done | bytes 1048608 | tf_op jit(solution)/shard_map/all_to_all | solution.py:20
  769.5 219.0 %while.30 = (s32[]{:T(128)}, f32[32,16,1024]{2,1,0:T(8,128)}, s32[32,16,1024]{2,1,0:T(8,128)}, f32[32,32,256]{2,1,0:T(8,128)S(1)}, s32[]{:T(128)}) while((s32[]{:T(128)}, f32[32,16,1024]{2,1,0:T(8,128)}, s32[32,16,1024]{2,1,0:T(8,128)}, f32[32,32,256]{2,1,0:T(8,128)S(1)}, s32[]{:T(128)}) %tuple.66), condition=%wide.region_10.11_spmd.clone, body=%wide.region_8.10_spmd.clone.sunk | while | flops 12566530 | bytes 1442369 | solution.py:104
  (196 shorter events, 514.8 us)
Async XLA Ops:
  7.4 721.3 %all-reduce.2.cloned.1.call-start = ((), (), s32[]{:S(2)}) async-start(), calls=%async_computation.3 | async-start | bytes 786432 | tf_op jit(solution)/shard_map/psum | solution.py:122
  14.0 453.7 %copy-start = (s32[1024]{0:T(1024)S(1)}, s32[1024]{0:T(1024)}, u32[]{:S(2)}) copy-start(s32[1024]{0:T(1024)} %param.13) | copy-start | bytes 12292
  473.2 256.6 %reduce-scatter.2.cloned.1.call-start = ((), (), s32[]{:S(2)}) async-start(), calls=%async_computation.2 | async-start | bytes 3244032 | tf_op jit(solution)/shard_map/reduce_scatter | solution.py:125
  736.6 32.9 %all-to-all-start = ((f32[32,32,256]{2,1,0:T(8,128)}), f32[32,32,256]{2,1,0:T(8,128)S(1)}, u32[]{:S(2)}, u32[]{:S(2)}) async-start(f32[32,32,256]{2,1,0:T(8,128)} %broadcast_in_dim.68), calls=%async_computation.1 | async-start | bytes 2097152 | tf_op jit(solution)/shard_map/all_to_all | solution.py:20
Sparse Core Ops, SparseCore 0:
  473.3 255.3 all-reduce.1
Sparse Core Ops, SparseCore 1:
  476.2 149.1 reduce-scatter.1
where the time goes:
time: 1000 us; the launch traced here: 996 us
  other arithmetic  606 us (61%)
  waiting for transfers between devices  280 us (28%)
  local copies, waits for them, and re-layouts  80.2 us (8%)
  between operations  14.9 us (1%)
    reduce_sum x32, other arithmetic, add_block(): return totals + jnp.sum(matches, axis=1, dtype=jnp.float32)  297 us
    psum x1, waiting for transfers between devices, body(): zone_counts = lax.psum(zone_part, ('tm', 'cells'))  253 us
    reduce_sum x32, other arithmetic, select_rows(): return jnp.sum(jnp.where(matches, lookup[None], 0.0), axis=2)  171 us
    add x32, other arithmetic, add_block(): return totals + jnp.sum(matches, axis=1, dtype=jnp.float32)  126 us
    dynamic_slice x32, local copies, waits for them, and re-layouts, add_block(): lax.dynamic_slice_in_dim(stacked, turn_index * day_block, day_block, 1)  30.1 us
    eq x32, local copies, waits for them, and re-layouts, select_rows(): matches = bins_rows[..., None] == levels  27 us
    all_to_all x1, waiting for transfers between devices, copy_for_each(): lax.all_to_all(jnp.broadcast_to(array[None], (count, *array.shape)), axis...  26.6 us
    dynamic_update_slice x32, local copies, waits for them, and re-layouts, apply_table(): return lax.map(select_rows, folded).reshape(day_count, cell_count)  20.5 us
  transfers between devices with their start and end apart: 3, of which 2 were waited for; matrix products, arithmetic and copies ran while one was open for 0% of the time, Pallas kernels for 0%

commit v1 on v0

--- a/solution.py
+++ b/solution.py
@@ -7,6 +7,7 @@
 BINS = 256
 REGIONS = 128
 pool_weight = 0.5
+clear_streams = lambda message: lax.psum(lax.psum(message, axis_name="cells"), axis_name="tm")
 
 
 def in_order(blocks, dim):
@@ -119,7 +120,7 @@
         precision=lax.Precision.HIGHEST,
         preferred_element_type=jnp.float32,
     )
-    zone_counts = lax.psum(zone_part, ("tm", "cells"))
+    zone_counts = clear_streams(zone_part)
     zone_share = zone_counts / jnp.sum(zone_counts, axis=2, keepdims=True)
     day_total = day_count * lax.axis_size("tm")
     share_rows = lax.psum_scatter(totals, "tm", scatter_dimension=1, tiled=True)

time: 1000 us -> 1280 us (1.28)
  waiting for transfers between devices: 280 us -> 549 us
    reduce_scatter x1, waiting for transfers between devices: 0.02 us -> 147 us  [body(): share_rows = lax.psum_scatter(totals, 'tm', scatter_dimension=1, tiled=True)]
    psum x1 -> x2, waiting for transfers between devices: 253 us -> 374 us  [the longest x1 267 us: lax.psum(lax.psum(message, axis_name='cells'), axis_name='tm')]
  transfers between devices with their start and end apart: 3 -> 4, of which waited for: 2 -> 4; matrix products, arithmetic and copies ran while one was open for 0% -> 0% of each run, Pallas kernels for 0% -> 0%
where the time goes in v1:
time: 1280 us; the launch traced here: 1270 us
  other arithmetic  613 us (48%)
  waiting for transfers between devices  549 us (43%)
  local copies, waits for them, and re-layouts  80.2 us (6%)
  between operations  13.2 us (1%)
    reduce_sum x32, other arithmetic, add_block(): return totals + jnp.sum(matches, axis=1, dtype=jnp.float32)  297 us
    psum x1, waiting for transfers between devices, lax.psum(lax.psum(message, axis_name='cells'), axis_name='tm')  267 us
    reduce_sum x32, other arithmetic, select_rows(): return jnp.sum(jnp.where(matches, lookup[None], 0.0), axis=2)  171 us
    reduce_scatter x1, waiting for transfers between devices, body(): share_rows = lax.psum_scatter(totals, 'tm', scatter_dimension=1, tiled=True)  147 us
    add x32, other arithmetic, add_block(): return totals + jnp.sum(matches, axis=1, dtype=jnp.float32)  133 us
    psum x1, waiting for transfers between devices, lax.psum(message, axis_name='cells')  108 us
    dynamic_slice x32, local copies, waits for them, and re-layouts, add_block(): lax.dynamic_slice_in_dim(stacked, turn_index * day_block, day_block, 1)  30.1 us
    eq x32, local copies, waits for them, and re-layouts, select_rows(): matches = bins_rows[..., None] == levels  27 us
  transfers between devices with their start and end apart: 4, of which 4 were waited for; matrix products, arithmetic and copies ran while one was open for 0% of the time, Pallas kernels for 0%

profile of v1, /device:TPU:1, one launch (start us, length us, event | category | flops | bytes accessed | tf_op | source)
XLA Modules:
  0.0 1272.8 jit_solution(1675923353319653063)
XLA Ops:
  13.2 460.2 %while.31 = (s32[]{:T(128)}, f32[3,1024,256]{2,1,0:T(8,128)}, s32[3,512,1024]{2,1,0:T(8,128)}, s32[]{:T(128)}, s32[]{:T(128)}, /*index=5*/s32[]{:T(128)}, s32[]{:T(128)}) while((s32[]{:T(128)}, f32[3,1024,256]{2,1,0:T(8,128)}, s32[3,512,1024]{2,1,0:T(8,128)}, s32[]{:T(128)}, s32[]{:T(128)}, /*index=5*/s32[]{:T(128)}, ...), condition=%wide.region_2.0_spmd.clone, body=%wide.region_0.0_spmd.clone.sunk | while | flops 51118084 | bytes 13172873 | solution.py:40
  14.1 9.3 convert_reduce_fusion.2
  26.7 9.3 convert_reduce_fusion.2
  41.1 9.3 convert_reduce_fusion.2
  55.6 9.3 convert_reduce_fusion.2
  70.0 9.3 convert_reduce_fusion.2
  84.4 9.3 convert_reduce_fusion.2
  98.9 9.3 convert_reduce_fusion.2
  113.3 9.3 convert_reduce_fusion.2
  127.8 9.3 convert_reduce_fusion.2
  142.2 9.3 convert_reduce_fusion.2
  156.6 9.3 convert_reduce_fusion.2
  171.1 9.3 convert_reduce_fusion.2
  185.5 9.3 convert_reduce_fusion.2
  200.0 9.3 convert_reduce_fusion.2
  214.4 9.3 convert_reduce_fusion.2
  228.8 9.3 convert_reduce_fusion.2
  358.8 9.3 convert_reduce_fusion.2
  478.8 107.6 %all-reduce.3.cloned.1.call-done = f32[3,128,256]{1,2,0:T(8,128)} async-done(((f32[3,128,256]{1,2,0:T(8,128)}), f32[3,128,256]{1,2,0:T(8,128)}) %all-reduce.3.cloned.1.call-update) | async-done | bytes 393232 | tf_op jit(solution)/shard_map/psum | solution.py:10
  588.9 266.9 %all-reduce.5.cloned.1.call-done = f32[3,128,256]{1,2,0:T(8,128)} async-done(((f32[3,128,256]{1,2,0:T(8,128)}), f32[3,128,256]{1,2,0:T(8,128)}) %all-reduce.5.cloned.1.call-update) | async-done | bytes 393232 | tf_op jit(solution)/shard_map/psum | solution.py:10
  856.9 147.4 %reduce-scatter.2.cloned.1.call-done = f32[3,32,256]{2,1,0:T(8,128)} async-done(((f32[3,1024,256]{2,1,0:T(8,128)}), f32[3,32,256]{2,1,0:T(8,128)}) %reduce-scatter.2.cloned.1.call-update) | async-done | bytes 98320 | tf_op jit(solution)/shard_map/reduce_scatter | solution.py:126
  1011.0 9.4 all-to-all-start
  1020.5 26.8 %all-to-all-done = f32[32,32,256]{2,1,0:T(8,128)S(1)} async-done(((f32[32,32,256]{2,1,0:T(8,128)}), f32[32,32,256]{2,1,0:T(8,128)S(1)}, u32[]{:S(2)}, u32[]{:S(2)}) %all-to-all-start) | async-done | bytes 1048608 | tf_op jit(solution)/shard_map/all_to_all | solution.py:21
  1047.2 219.0 %while.30 = (s32[]{:T(128)}, f32[32,16,1024]{2,1,0:T(8,128)}, s32[32,16,1024]{2,1,0:T(8,128)}, f32[32,32,256]{2,1,0:T(8,128)S(1)}, s32[]{:T(128)}) while((s32[]{:T(128)}, f32[32,16,1024]{2,1,0:T(8,128)}, s32[32,16,1024]{2,1,0:T(8,128)}, f32[32,32,256]{2,1,0:T(8,128)S(1)}, s32[]{:T(128)}) %tuple.68), condition=%wide.region_11.12_spmd.clone, body=%wide.region_9.11_spmd.clone.sunk | while | flops 12566530 | bytes 1442369 | solution.py:105
  (199 shorter events, 543.0 us)
Async XLA Ops:
  6.5 579.9 %all-reduce.3.cloned.1.call-start = ((), (), s32[]{:S(2)}) async-start(), calls=%async_computation.3 | async-start | bytes 786432 | tf_op jit(solution)/shard_map/psum | solution.py:10
  13.2 460.2 %copy-start = (s32[1024]{0:T(1024)S(1)}, s32[1024]{0:T(1024)}, u32[]{:S(2)}) copy-start(s32[1024]{0:T(1024)} %param.13) | copy-start | bytes 12292
  478.8 377.0 %all-reduce.5.cloned.1.call-start = ((), (), s32[]{:S(2)}) async-start(), calls=%async_computation.4 | async-start | bytes 786432 | tf_op jit(solution)/shard_map/psum | solution.py:10
  586.4 417.8 %reduce-scatter.2.cloned.1.call-start = ((), (), s32[]{:S(2)}) async-start(), calls=%async_computation.2 | async-start | bytes 3244032 | tf_op jit(solution)/shard_map/reduce_scatter | solution.py:126
  1011.0 36.2 %all-to-all-start = ((f32[32,32,256]{2,1,0:T(8,128)}), f32[32,32,256]{2,1,0:T(8,128)S(1)}, u32[]{:S(2)}, u32[]{:S(2)}) async-start(f32[32,32,256]{2,1,0:T(8,128)} %broadcast_in_dim.68), calls=%async_computation.1 | async-start | bytes 2097152 | tf_op jit(solution)/shard_map/all_to_all | solution.py:21
Sparse Core Ops, SparseCore 0:
  478.9 107.4 all-reduce.2
  589.0 266.7 all-reduce.4
  858.3 145.8 reduce-scatter.1
